TPU v7x, 256 devices: a whole 4x4x8 slice. The times are simulated.
256 devices in a mesh: ent: 64 (over z, y, core), rel: 4 (over x).
Axes of the slice: x: 4, y: 4, z: 8, core: 2. Of those that a mesh axis runs over, the one named last changes fastest.
Arguments:
- entity_rows: bfloat16 [65536, 256], P('ent'), may hold values from -2.5 to 2.5
- request_rows: int32 [64, 64, 32], P('ent'), may hold values from 0 to 1023
- edge_heads: int32 [262144], P(('ent', 'rel')), may hold values from 0 to 1023
- edge_rels: int32 [262144], P(('ent', 'rel')), may hold values from 0 to 7
- edge_tails: int32 [262144], P(('ent', 'rel')), may hold values from 0 to 2047
- edge_counts: int32 [256], P(('ent', 'rel')), may hold values from 1 to 1024, 163840 in all
- negative_rows: int32 [65536], P(('ent', 'rel')), may hold values from 0 to 1023
- relation_blocks: bfloat16 [32, 8, 32, 32], P('rel'), may hold values from -1 to 1
Outputs:
- entity_grad: float32 [65536, 256], P('ent')
- relation_grad: float32 [32, 8, 32, 32], P('rel')
Inputs may be any that keep to these rules, and one draw needn't show every extreme that they name: Edge slots of bucket b at or past edge_counts[b] are ignored; some bucket is full in every draw.
All inputs are finite; a program needn't handle non-finite values. No bound on the sum of `edge_counts` on one device may be relied on, other than what follows from the above.
Results may differ from a plain program's by a relative error of at most 0.009.
Values may be sent and summed in bfloat16 or wider, within the bound.
No kernel may reach another device: no remote copies, remote signals or barrier semaphores. Data moves between devices by JAX's collectives and lax.ppermute only.
A program may use at most 64 MiB of HBM per device.

v0:
```python
import math
import jax
import jax.numpy as jnp
from jax import lax
from jax.sharding import PartitionSpec as P


def pick_rows(indices, source_table):
    row_total = indices.shape[0]
    block_size = math.gcd(row_total, 256)
    grouped = indices.reshape(row_total // block_size, block_size)
    columns = jnp.arange(source_table.shape[0], dtype=jnp.int32)

    def pick_block(index_block):
        one_hot = (index_block[:, None] == columns[None, :]).astype(jnp.bfloat16)
        return jnp.dot(one_hot, source_table, preferred_element_type=jnp.float32).astype(
            jnp.bfloat16
        )

    picked = lax.map(pick_block, grouped)
    return picked.reshape(row_total, source_table.shape[1])


def owner_add(indices, gradients, entity_count):
    start_value = jnp.zeros((entity_count, gradients.shape[1]), jnp.float32)
    return start_value.at[indices].add(gradients)


def local(
    entity_rows,
    request_rows,
    edge_heads,
    edge_rels,
    edge_tails,
    edge_counts,
    negative_rows,
    relation_blocks,
):
    entity_count, feature_width = entity_rows.shape
    part_count = request_rows.shape[1]
    slot_count = request_rows.shape[2]
    r_count, block_count, block_width = (
        relation_blocks.shape[0],
        relation_blocks.shape[1],
        relation_blocks.shape[2],
    )
    neg_count = negative_rows.shape[0]
    owner_lists = lax.all_to_all(request_rows, "ent", split_axis=1, concat_axis=0, tiled=True)
    wanted = pick_rows(owner_lists.reshape(-1), entity_rows).reshape(
        part_count, 1, slot_count, feature_width
    )
    fetched = lax.all_to_all(wanted, "ent", split_axis=0, concat_axis=1, tiled=True)
    fetched = fetched.reshape(part_count * slot_count, feature_width)
    neg_rows = pick_rows(negative_rows, entity_rows)
    edge_dev = edge_heads.shape[0]
    block_size = math.gcd(edge_dev, 256)
    block_total = edge_dev // block_size
    live_count = edge_counts[0]
    positions = jnp.arange(edge_dev, dtype=jnp.int32).reshape(block_total, block_size)
    entity_columns = jnp.arange(entity_count, dtype=jnp.int32)
    slot_columns = jnp.arange(part_count * slot_count, dtype=jnp.int32)
    rel_columns = jnp.arange(r_count, dtype=jnp.int32)
    contract_rows = (((0,), (0,)), ((), ()))

    def edge_block(running, block_inputs):
        slot_acc, entity_acc, neg_acc, relation_acc = running
        head_ids, rel_ids, tail_ids, places = block_inputs
        live_mask = (places < live_count).astype(jnp.float32)
        head_hot = (head_ids[:, None] == entity_columns[None, :]).astype(jnp.bfloat16)
        tail_hot = (tail_ids[:, None] == slot_columns[None, :]).astype(jnp.bfloat16)
        head_rows = jnp.dot(head_hot, entity_rows, preferred_element_type=jnp.float32).astype(
            jnp.bfloat16
        )
        tail_rows = jnp.dot(tail_hot, fetched, preferred_element_type=jnp.float32).astype(
            jnp.bfloat16
        )
        rel_hot = (rel_ids[:, None] == rel_columns[None, :]).astype(jnp.float32)
        head_split = head_rows.reshape(block_size, block_count, block_width)
        proj_all = jnp.einsum(
            "enb,rnbc->renc", head_split, relation_blocks, preferred_element_type=jnp.float32
        )
        projected = (
            jnp.sum(rel_hot.T[:, :, None, None] * proj_all, 0)
            .reshape(block_size, feature_width)
            .astype(jnp.bfloat16)
        )
        projected_wide = projected.astype(jnp.float32)
        positive = jnp.sum(projected_wide * tail_rows.astype(jnp.float32), -1)
        negative = lax.dot_general(
            projected, neg_rows, (((1,), (1,)), ((), ())), preferred_element_type=jnp.float32
        )
        pos_weight = -live_mask * jax.nn.sigmoid(-positive)
        neg_weight = (live_mask[:, None] * jax.nn.sigmoid(negative) / neg_count).astype(
            jnp.bfloat16
        )
        grad_proj = (
            pos_weight[:, None] * tail_rows.astype(jnp.float32)
            + jnp.dot(neg_weight, neg_rows, preferred_element_type=jnp.float32)
        ).astype(jnp.bfloat16)
        weighted = (pos_weight[:, None] * projected_wide).astype(jnp.bfloat16)
        grad_split = grad_proj.reshape(block_size, block_count, block_width)
        back_all = jnp.einsum(
            "enc,rnbc->renb", grad_split, relation_blocks, preferred_element_type=jnp.float32
        )
        head_grad = (
            jnp.sum(rel_hot.T[:, :, None, None] * back_all, 0)
            .reshape(block_size, feature_width)
            .astype(jnp.bfloat16)
        )
        slot_acc = slot_acc + lax.dot_general(
            tail_hot, weighted, contract_rows, preferred_element_type=jnp.float32
        )
        entity_acc = entity_acc + lax.dot_general(
            head_hot, head_grad, contract_rows, preferred_element_type=jnp.float32
        )
        neg_acc = neg_acc + lax.dot_general(
            neg_weight, projected, contract_rows, preferred_element_type=jnp.float32
        )
        masked_heads = rel_hot.T.astype(jnp.bfloat16)[:, :, None, None] * head_split[None]
        relation_acc = relation_acc + jnp.einsum(
            "renb,enc->rnbc", masked_heads, grad_split, preferred_element_type=jnp.float32
        )
        return ((slot_acc, entity_acc, neg_acc, relation_acc), None)

    start_values = (
        jnp.zeros((part_count * slot_count, feature_width), jnp.float32),
        jnp.zeros((entity_count, feature_width), jnp.float32),
        jnp.zeros((neg_count, feature_width), jnp.float32),
        jnp.zeros(relation_blocks.shape, jnp.float32),
    )
    block_inputs = (
        edge_heads.reshape(block_total, block_size),
        edge_rels.reshape(block_total, block_size),
        edge_tails.reshape(block_total, block_size),
        positions,
    )
    (slot_acc, entity_acc, neg_acc, relation_acc), _ = lax.scan(
        edge_block, start_values, block_inputs
    )
    neg_hot = (negative_rows[:, None] == entity_columns[None, :]).astype(jnp.bfloat16)
    entity_acc = entity_acc + lax.dot_general(
        neg_hot, neg_acc.astype(jnp.bfloat16), contract_rows, preferred_element_type=jnp.float32
    )
    slot_grads = slot_acc.reshape(1, part_count, slot_count, feature_width)
    returned = lax.all_to_all(
        slot_grads.astype(jnp.bfloat16), "ent", split_axis=1, concat_axis=0, tiled=True
    ).astype(slot_grads.dtype)
    entity_acc = entity_acc + owner_add(
        owner_lists.reshape(-1), returned.reshape(-1, feature_width), entity_count
    )
    entity_grad = lax.psum(entity_acc, "rel")
    relation_grad = lax.psum(relation_acc, "ent")
    return (entity_grad, relation_grad)


def solution(mesh):
    in_specs = (
        P("ent", None),
        P("ent", None, None),
        P(("ent", "rel")),
        P(("ent", "rel")),
        P(("ent", "rel")),
        P(("ent", "rel")),
        P(("ent", "rel")),
        P("rel", None, None, None),
    )
    out_specs = (P("ent", None), P("rel", None, None, None))
    return jax.shard_map(local, mesh=mesh, in_specs=in_specs, out_specs=out_specs, check_vma=False)
```

profile of v0, /device:TPU:8, one launch (start us, length us, event | category | flops | bytes accessed | tf_op | source)
XLA Modules:
  0.0 383.0 jit_solution(16212449031649504692)
XLA Ops:
  7.2 1.4 copy.20
  8.6 12.1 %all-to-all-start = ((s32[1,64,32]{2,0,1:T(1,128)}), s32[1,64,32]{2,0,1:T(1,128)S(1)}, u32[]{:S(2)}, u32[]{:S(2)}) async-start(s32[1,64,32]{2,0,1:T(1,128)} %copy.20), calls=%async_computation | async-start | bytes 65536 | tf_op jit(solution)/shard_map/all_to_all | solution.py:48
  20.7 8.5 %all-to-all-done = s32[1,64,32]{2,0,1:T(1,128)S(1)} async-done(((s32[1,64,32]{2,0,1:T(1,128)}), s32[1,64,32]{2,0,1:T(1,128)S(1)}, u32[]{:S(2)}, u32[]{:S(2)}) %all-to-all-start) | async-done | bytes 8224 | tf_op jit(solution)/shard_map/all_to_all | solution.py:48
  29.8 0.7 reduce.5
  30.6 16.5 %while.32 = (s32[]{:T(128)}, bf16[8,256,256]{2,1,0:T(8,128)(2,1)}, s32[8,256]{1,0:T(8,128)S(1)}, bf16[1024,256]{1,0:T(8,128)(2,1)}, s32[]{:T(128)}) while((s32[]{:T(128)}, bf16[8,256,256]{2,1,0:T(8,128)(2,1)}, s32[8,256]{1,0:T(8,128)S(1)}, bf16[1024,256]{1,0:T(8,128)(2,1)}, s32[]{:T(128)}) %tuple.56), condition=%wide.region_1.2_spmd.clone, body=%wide.region_0.1_spmd.clone.sunk | while | flops 134545408 | bytes 658509 | solution.py:20
  30.6 2.1 fusion.90
  32.6 2.0 fusion.90
  34.7 2.0 fusion.90
  36.8 2.1 fusion.90
  38.8 2.1 fusion.90
  40.9 2.0 fusion.90
  42.9 2.0 fusion.90
  45.0 2.1 fusion.90
  47.0 6.5 %all-to-all-start.1 = ((bf16[64,1,32,256]{3,2,1,0:T(8,128)(2,1)}), bf16[64,1,32,256]{3,2,1,0:T(8,128)(2,1)}, u32[]{:S(2)}, u32[]{:S(2)}) async-start(bf16[64,1,32,256]{3,2,1,0:T(8,128)(2,1)} %bitcast.1), calls=%async_computation.1 | async-start | bytes 2097152 | tf_op jit(solution)/shard_map/all_to_all | solution.py:52
  53.6 1.9 copy.21
  55.5 1.4 convolution_convert_fusion.2
  56.9 25.4 %all-to-all-done.1 = bf16[64,1,32,256]{3,2,1,0:T(8,128)(2,1)} async-done(((bf16[64,1,32,256]{3,2,1,0:T(8,128)(2,1)}), bf16[64,1,32,256]{3,2,1,0:T(8,128)(2,1)}, u32[]{:S(2)}, u32[]{:S(2)}) %all-to-all-start.1) | async-done | bytes 1048608 | tf_op jit(solution)/shard_map/all_to_all | solution.py:52
  82.3 38.9 %while.33 = (s32[]{:T(128)}, f32[2048,256]{1,0:T(8,128)S(1)}, f32[1024,256]{1,0:T(8,128)S(1)}, f32[256,256]{1,0:T(8,128)S(1)}, f32[8,8,32,32]{2,3,0,1:T(8,128)},...) while((s32[]{:T(128)}, f32[2048,256]{1,0:T(8,128)S(1)}, ...), condition=%wide.region_6.7_spmd.clone, body=%wide.region_2.6_spmd.clone.sunk | while | flops 1016077568 | bytes 14733582 | solution.py:137
  83.0 1.5 convolution_convert_fusion.4
  84.5 1.5 fusion.110
  86.6 2.1 fusion.111
  89.4 0.9 fusion.115
  90.9 1.1 convolution_add_fusion.8
  92.8 1.5 convolution_convert_fusion.4
  94.3 1.5 fusion.110
  96.4 2.1 fusion.111
  99.1 0.9 fusion.115
  100.7 1.1 convolution_add_fusion.8
  102.5 1.5 convolution_convert_fusion.4
  104.0 1.5 fusion.110
  106.1 2.1 fusion.111
  108.9 0.9 fusion.115
  110.4 1.1 convolution_add_fusion.8
  112.2 1.5 convolution_convert_fusion.4
  113.7 1.5 fusion.110
  115.8 2.1 fusion.111
  118.6 0.9 fusion.115
  120.2 1.1 convolution_add_fusion.8
  121.2 1.1 convert_element_type.106
  122.3 5.9 %all-to-all-start.2 = ((bf16[1,64,32,256]{3,2,0,1:T(8,128)(2,1)}), bf16[1,64,32,256]{3,2,0,1:T(8,128)(2,1)S(1)}, u32[]{:S(2)}, u32[]{:S(2)}) async-start(bf16[1,64,32,256]{3,2,0,1:T(8,128)(2,1)} %bitcast.124), calls=%async_computation.2 | async-start | bytes 2097152 | tf_op jit(solution)/shard_map/all_to_all | solution.py:145
  128.4 1.4 copy.22
  130.4 27.4 %all-to-all-done.2 = bf16[1,64,32,256]{3,2,0,1:T(8,128)(2,1)S(1)} async-done(((bf16[1,64,32,256]{3,2,0,1:T(8,128)(2,1)}), bf16[1,64,32,256]{3,2,0,1:T(8,128)(2,1)S(1)}, u32[]{:S(2)}, u32[]{:S(2)}) %all-to-all-start.2) | async-done | bytes 1048608 | tf_op jit(solution)/shard_map/all_to_all | solution.py:145
  157.7 12.0 %scatter_custom_fusion = f32[1024,256]{1,0:T(8,128)S(1)} fusion(f32[1024,256]{1,0:T(8,128)S(1)} %convolution_add_fusion.4, s32[2048]{0:T(1024)S(1)} %bitcast.138, bf16[2048,256]{1,0:T(8,128)(2,1)S(1)} %bitcast.125), kind=kCustom, calls=%fused_computation.57 | custom fusion | flops 1048576 | bytes 2097152 | tf_op jit(solution)/shard_map/scatter-add | solution.py:26
  169.8 1.0 copy-done.3
  170.8 150.9 %all-reduce.5.cloned.1.call-done = f32[8,8,32,32]{3,2,1,0:T(8,128)} async-done(((f32[8,8,32,32]{3,2,1,0:T(8,128)}), f32[8,8,32,32]{3,2,1,0:T(8,128)}) %all-reduce.5.cloned.1.call-update) | async-done | bytes 262160 | tf_op jit(solution)/shard_map/psum | solution.py:152
  321.6 51.3 %all-reduce.3.cloned.1.call-done = f32[1024,256]{1,0:T(8,128)} async-done(((f32[1024,256]{1,0:T(8,128)}), f32[1024,256]{1,0:T(8,128)}) %all-reduce.3.cloned.1.call-update) | async-done | bytes 1048592 | tf_op jit(solution)/shard_map/psum | solution.py:151
  372.9 2.3 copy.51
  375.2 1.0 copy.52
  (107 shorter events, 11.3 us)
Async XLA Ops:
  8.6 20.7 %all-to-all-start = ((s32[1,64,32]{2,0,1:T(1,128)}), s32[1,64,32]{2,0,1:T(1,128)S(1)}, u32[]{:S(2)}, u32[]{:S(2)}) async-start(s32[1,64,32]{2,0,1:T(1,128)} %copy.20), calls=%async_computation | async-start | bytes 65536 | tf_op jit(solution)/shard_map/all_to_all | solution.py:48
  29.2 1.3 copy-start.6
  47.0 6.5 %copy-start.8 = (s32[1024]{0:T(1024)S(1)}, s32[1024]{0:T(1024)}, u32[]{:S(2)}) copy-start(s32[1024]{0:T(1024)} %param.14) | copy-start | bytes 12292
  47.0 6.5 %copy-start.9 = (s32[1024]{0:T(1024)S(1)}, s32[1024]{0:T(1024)}, u32[]{:S(2)}) copy-start(s32[1024]{0:T(1024)} %param.15) | copy-start | bytes 12292
  47.0 6.6 %copy-start.10 = (s32[1024]{0:T(1024)S(1)}, s32[1024]{0:T(1024)}, u32[]{:S(2)}) copy-start(s32[1024]{0:T(1024)} %param.16) | copy-start | bytes 12292
  47.0 35.3 %all-to-all-start.1 = ((bf16[64,1,32,256]{3,2,1,0:T(8,128)(2,1)}), bf16[64,1,32,256]{3,2,1,0:T(8,128)(2,1)}, u32[]{:S(2)}, u32[]{:S(2)}) async-start(bf16[64,1,32,256]{3,2,1,0:T(8,128)(2,1)} %bitcast.1), calls=%async_computation.1 | async-start | bytes 2097152 | tf_op jit(solution)/shard_map/all_to_all | solution.py:52
  86.4 2.6 copy-start.5
  86.6 2.8 copy-start
  90.4 1.7 copy-start.1
  96.1 2.6 copy-start.5
  96.4 2.8 copy-start
  100.1 1.7 copy-start.1
  105.8 2.6 copy-start.5
  106.1 2.8 copy-start
  109.8 1.7 copy-start.1
  115.6 2.6 copy-start.5
  115.8 2.8 copy-start
  119.6 1.7 copy-start.1
  121.2 7.0 %copy-start.7 = (s32[1,64,32]{2,0,1:T(1,128)S(1)}, s32[1,64,32]{2,0,1:T(1,128)}, u32[]{:S(2)}) copy-start(s32[1,64,32]{2,0,1:T(1,128)} %copy-done.6) | copy-start | bytes 24580
  122.3 6.0 %copy-start.2 = (f32[8,8,32,32]{2,3,0,1:T(8,128)S(1)}, f32[8,8,32,32]{2,3,0,1:T(8,128)}, u32[]{:S(2)}) copy-start(f32[8,8,32,32]{2,3,0,1:T(8,128)} %get-tuple-element.138) | copy-start | bytes 786436
  122.3 35.4 %all-to-all-start.2 = ((bf16[1,64,32,256]{3,2,0,1:T(8,128)(2,1)}), bf16[1,64,32,256]{3,2,0,1:T(8,128)(2,1)S(1)}, u32[]{:S(2)}, u32[]{:S(2)}) async-start(bf16[1,64,32,256]{3,2,0,1:T(8,128)(2,1)} %bitcast.124), calls=%async_computation.2 | async-start | bytes 2097152 | tf_op jit(solution)/shard_map/all_to_all | solution.py:145
  128.2 1.6 copy-start.11
  128.2 193.4 %all-reduce.5.cloned.1.call-start = ((), (), s32[]{:S(2)}) async-start(), calls=%async_computation.4 | async-start | bytes 2097152 | tf_op jit(solution)/shard_map/psum | solution.py:152
  129.8 243.2 %all-reduce.3.cloned.1.call-start = ((), (), s32[]{:S(2)}) async-start(), calls=%async_computation.3 | async-start | bytes 2097152 | tf_op jit(solution)/shard_map/psum | solution.py:151
  169.8 1.0 copy-start.3
  321.6 53.6 %copy-start.4 = (f32[8,8,32,32]{3,2,1,0:T(8,128)S(1)}, f32[8,8,32,32]{3,2,1,0:T(8,128)}, u32[]{:S(2)}) copy-start(f32[8,8,32,32]{3,2,1,0:T(8,128)} %all-reduce.5.cloned.1.call-done) | copy-start | bytes 786436
Sparse Core Ops, SparseCore 0:
  132.4 189.1 all-reduce.4
  324.6 48.3 all-reduce.2
where the time goes:
time: 384 us; the launch traced here: 383 us
  waiting for transfers between devices  263 us (68%)
  matrix products  53.8 us (14%)
  starting transfers between devices  24.5 us (6%)
  other arithmetic  16.5 us (4%)
  between operations  14.2 us (4%)
  local copies, waits for them, and re-layouts  9.81 us (3%)
    psum x1, waiting for transfers between devices, local(): relation_grad = lax.psum(relation_acc, 'ent')  151 us
    psum x1, waiting for transfers between devices, local(): entity_grad = lax.psum(entity_acc, 'rel')  51.3 us
    all_to_all x1, waiting for transfers between devices, local(): lax.all_to_all(slot_grads.astype(jnp.bfloat16), 'ent', split_axis=1, conc...  27.4 us
    all_to_all x1, waiting for transfers between devices, local(): lax.all_to_all(wanted, 'ent', split_axis=0, concat_axis=1, tiled=True)  25.4 us
    dot_general x9, matrix products, pick_block(): jnp.dot(one_hot, source_table, preferred_element_type=jnp.float32)  17.8 us
    all_to_all x1, starting transfers between devices, local(): lax.all_to_all(request_rows, 'ent', split_axis=1, concat_axis=0, tiled=True)  12.1 us
    scatter-add x1, other arithmetic, owner_add(): return start_value.at[indices].add(gradients)  12 us
    all_to_all x1, waiting for transfers between devices, local(): lax.all_to_all(request_rows, 'ent', split_axis=1, concat_axis=0, tiled=True)  8.54 us
  transfers between devices with their start and end apart: 5, of which 5 were waited for; matrix products, arithmetic and copies ran while one was open for 5% of the time, Pallas kernels for 0%

commit v1 on v0

--- a/solution.py
+++ b/solution.py
@@ -142,8 +142,16 @@
         neg_hot, neg_acc.astype(jnp.bfloat16), contract_rows, preferred_element_type=jnp.float32
     )
     slot_grads = slot_acc.reshape(1, part_count, slot_count, feature_width)
-    returned = lax.all_to_all(
-        slot_grads.astype(jnp.bfloat16), "ent", split_axis=1, concat_axis=0, tiled=True
+    returned = jnp.concatenate(
+        jax.lax.all_to_all(
+            jnp.stack(
+                jnp.split(slot_grads.astype(jnp.bfloat16), jax.lax.axis_size("ent"), 1), axis=0
+            ),
+            "ent",
+            0,
+            0,
+        ),
+        0,
     ).astype(slot_grads.dtype)
     entity_acc = entity_acc + owner_add(
         owner_lists.reshape(-1), returned.reshape(-1, feature_width), entity_count

time: 384 us -> 422 us (1.099)
  local copies, waits for them, and re-layouts: 9.81 us -> 48.6 us
    unnamed x22 -> x85, local copies, waits for them, and re-layouts: 7.54 us -> 45.7 us
  transfers between devices with their start and end apart: 5 -> 5, of which waited for: 5 -> 5; matrix products, arithmetic and copies ran while one was open for 5% -> 4% of each run, Pallas kernels for 0% -> 0%
where the time goes in v1:
time: 422 us; the launch traced here: 421 us
  waiting for transfers between devices  263 us (62%)
  matrix products  53.8 us (13%)
  local copies, waits for them, and re-layouts  48.6 us (12%)
  starting transfers between devices  24.4 us (6%)
  other arithmetic  15.7 us (4%)
  between operations  14.3 us (3%)
    psum x1, waiting for transfers between devices, local(): relation_grad = lax.psum(relation_acc, 'ent')  151 us
    psum x1, waiting for transfers between devices, local(): entity_grad = lax.psum(entity_acc, 'rel')  51.3 us
    unnamed x85, local copies, waits for them, and re-layouts  45.7 us
    all_to_all x1, waiting for transfers between devices, local(): jax.lax.all_to_all(jnp.stack(jnp.split(slot_grads.astype(jnp.bfloat16), j...  27.4 us
    all_to_all x1, waiting for transfers between devices, local(): lax.all_to_all(wanted, 'ent', split_axis=0, concat_axis=1, tiled=True)  25.4 us
    dot_general x9, matrix products, pick_block(): jnp.dot(one_hot, source_table, preferred_element_type=jnp.float32)  17.8 us
    scatter-add x1, other arithmetic, owner_add(): return start_value.at[indices].add(gradients)  12.2 us
    all_to_all x1, starting transfers between devices, local(): lax.all_to_all(request_rows, 'ent', split_axis=1, concat_axis=0, tiled=True)  12.1 us
  transfers between devices with their start and end apart: 5, of which 5 were waited for; matrix products, arithmetic and copies ran while one was open for 4% of the time, Pallas kernels for 0%

profile of v1, /device:TPU:8, one launch (start us, length us, event | category | flops | bytes accessed | tf_op | source)
XLA Modules:
  0.0 420.8 jit_solution(12543262863781457874)
XLA Ops:
  7.2 1.4 copy.146
  8.6 12.1 %all-to-all-start = ((s32[1,64,32]{2,0,1:T(1,128)}), s32[1,64,32]{2,0,1:T(1,128)S(1)}, u32[]{:S(2)}, u32[]{:S(2)}) async-start(s32[1,64,32]{2,0,1:T(1,128)} %copy.146), calls=%async_computation | async-start | bytes 65536 | tf_op jit(solution)/shard_map/all_to_all | solution.py:48
  20.7 8.5 %all-to-all-done = s32[1,64,32]{2,0,1:T(1,128)S(1)} async-done(((s32[1,64,32]{2,0,1:T(1,128)}), s32[1,64,32]{2,0,1:T(1,128)S(1)}, u32[]{:S(2)}, u32[]{:S(2)}) %all-to-all-start) | async-done | bytes 8224 | tf_op jit(solution)/shard_map/all_to_all | solution.py:48
  29.8 0.7 reduce.5
  30.6 16.5 %while.32 = (s32[]{:T(128)}, bf16[8,256,256]{2,1,0:T(8,128)(2,1)}, s32[8,256]{1,0:T(8,128)S(1)}, bf16[1024,256]{1,0:T(8,128)(2,1)}, s32[]{:T(128)}) while((s32[]{:T(128)}, bf16[8,256,256]{2,1,0:T(8,128)(2,1)}, s32[8,256]{1,0:T(8,128)S(1)}, bf16[1024,256]{1,0:T(8,128)(2,1)}, s32[]{:T(128)}) %tuple.56), condition=%wide.region_1.2_spmd.clone, body=%wide.region_0.1_spmd.clone.sunk | while | flops 134545408 | bytes 658509 | solution.py:20
  30.6 2.1 fusion.90
  32.6 2.1 fusion.90
  34.7 2.1 fusion.90
  36.8 2.0 fusion.90
  38.8 2.0 fusion.90
  40.9 2.1 fusion.90
  42.9 2.1 fusion.90
  45.0 2.0 fusion.90
  47.0 6.5 %all-to-all-start.1 = ((bf16[64,1,32,256]{3,2,1,0:T(8,128)(2,1)}), bf16[64,1,32,256]{3,2,1,0:T(8,128)(2,1)}, u32[]{:S(2)}, u32[]{:S(2)}) async-start(bf16[64,1,32,256]{3,2,1,0:T(8,128)(2,1)} %bitcast.1), calls=%async_computation.1 | async-start | bytes 2097152 | tf_op jit(solution)/shard_map/all_to_all | solution.py:52
  53.6 1.9 copy.147
  55.5 1.4 convolution_convert_fusion.2
  56.9 25.4 %all-to-all-done.1 = bf16[64,1,32,256]{3,2,1,0:T(8,128)(2,1)} async-done(((bf16[64,1,32,256]{3,2,1,0:T(8,128)(2,1)}), bf16[64,1,32,256]{3,2,1,0:T(8,128)(2,1)}, u32[]{:S(2)}, u32[]{:S(2)}) %all-to-all-start.1) | async-done | bytes 1048608 | tf_op jit(solution)/shard_map/all_to_all | solution.py:52
  82.3 38.9 %while.33 = (s32[]{:T(128)}, f32[2048,256]{1,0:T(8,128)S(1)}, f32[1024,256]{1,0:T(8,128)S(1)}, f32[256,256]{1,0:T(8,128)S(1)}, f32[8,8,32,32]{2,3,0,1:T(8,128)},...) while((s32[]{:T(128)}, f32[2048,256]{1,0:T(8,128)S(1)}, ...), condition=%wide.region_6.7_spmd.clone, body=%wide.region_2.6_spmd.clone.sunk | while | flops 1016077568 | bytes 14733582 | solution.py:137
  83.0 1.5 convolution_convert_fusion.4
  84.5 1.5 fusion.110
  86.6 2.1 fusion.111
  89.4 0.9 fusion.115
  90.9 1.1 convolution_add_fusion.8
  92.0 0.7 compare_convert_fusion.2
  92.8 1.5 convolution_convert_fusion.4
  94.3 1.5 fusion.110
  96.4 2.1 fusion.111
  99.1 0.9 fusion.115
  100.7 1.1 convolution_add_fusion.8
  102.5 1.5 convolution_convert_fusion.4
  104.0 1.5 fusion.110
  106.1 2.1 fusion.111
  108.9 0.9 fusion.115
  110.4 1.1 convolution_add_fusion.8
  112.2 1.5 convolution_convert_fusion.4
  113.7 1.5 fusion.110
  115.8 2.1 fusion.111
  118.6 0.9 fusion.115
  120.2 1.1 convolution_add_fusion.8
  160.2 5.7 %all-to-all-start.2 = ((bf16[64,1,1,32,256]{4,3,2,1,0:T(8,128)(2,1)}), bf16[64,1,1,32,256]{4,3,2,1,0:T(8,128)(2,1)S(1)}, u32[]{:S(2)}, u32[]{:S(2)}) async-start(bf16[64,1,1,32,256]{4,3,2,1,0:T(8,128)(2,1)} %constant_dynamic-update-slice_fusion), calls=%async_computation.2 | async-start | bytes 2097152 | tf_op jit(solution)/shard_map/all_to_all | solution.py:146
  166.1 1.4 copy.148
  168.1 27.4 %all-to-all-done.2 = bf16[64,1,1,32,256]{4,3,2,1,0:T(8,128)(2,1)S(1)} async-done(((bf16[64,1,1,32,256]{4,3,2,1,0:T(8,128)(2,1)}), bf16[64,1,1,32,256]{4,3,2,1,0:T(8,128)(2,1)S(1)}, u32[]{:S(2)}, u32[]{:S(2)}) %all-to-all-start.2) | async-done | bytes 1048608 | tf_op jit(solution)/shard_map/all_to_all | solution.py:146
  195.5 12.2 %scatter_custom_fusion = f32[1024,256]{1,0:T(8,128)S(1)} fusion(f32[1024,256]{1,0:T(8,128)S(1)} %convolution_add_fusion.4, s32[2048]{0:T(1024)S(1)} %bitcast.457, bf16[2048,256]{1,0:T(8,128)(2,1)S(1)} %bitcast.380), kind=kCustom, calls=%fused_computation.57 | custom fusion | flops 1048576 | bytes 2097152 | tf_op jit(solution)/shard_map/scatter-add | solution.py:26
  207.7 1.0 copy-done.3
  208.7 150.7 %all-reduce.5.cloned.1.call-done = f32[8,8,32,32]{3,2,1,0:T(8,128)} async-done(((f32[8,8,32,32]{3,2,1,0:T(8,128)}), f32[8,8,32,32]{3,2,1,0:T(8,128)}) %all-reduce.5.cloned.1.call-update) | async-done | bytes 262160 | tf_op jit(solution)/shard_map/psum | solution.py:160
  359.4 51.3 %all-reduce.3.cloned.1.call-done = f32[1024,256]{1,0:T(8,128)} async-done(((f32[1024,256]{1,0:T(8,128)}), f32[1024,256]{1,0:T(8,128)}) %all-reduce.3.cloned.1.call-update) | async-done | bytes 1048592 | tf_op jit(solution)/shard_map/psum | solution.py:159
  410.7 2.3 copy.240
  413.0 1.0 copy.241
  (171 shorter events, 49.6 us)
Async XLA Ops:
  8.6 20.7 %all-to-all-start = ((s32[1,64,32]{2,0,1:T(1,128)}), s32[1,64,32]{2,0,1:T(1,128)S(1)}, u32[]{:S(2)}, u32[]{:S(2)}) async-start(s32[1,64,32]{2,0,1:T(1,128)} %copy.146), calls=%async_computation | async-start | bytes 65536 | tf_op jit(solution)/shard_map/all_to_all | solution.py:48
  29.2 1.3 copy-start.6
  47.0 6.5 %copy-start.8 = (s32[1024]{0:T(1024)S(1)}, s32[1024]{0:T(1024)}, u32[]{:S(2)}) copy-start(s32[1024]{0:T(1024)} %param.14) | copy-start | bytes 12292
  47.0 6.5 %copy-start.9 = (s32[1024]{0:T(1024)S(1)}, s32[1024]{0:T(1024)}, u32[]{:S(2)}) copy-start(s32[1024]{0:T(1024)} %param.15) | copy-start | bytes 12292
  47.0 6.6 %copy-start.10 = (s32[1024]{0:T(1024)S(1)}, s32[1024]{0:T(1024)}, u32[]{:S(2)}) copy-start(s32[1024]{0:T(1024)} %param.16) | copy-start | bytes 12292
  47.0 35.3 %all-to-all-start.1 = ((bf16[64,1,32,256]{3,2,1,0:T(8,128)(2,1)}), bf16[64,1,32,256]{3,2,1,0:T(8,128)(2,1)}, u32[]{:S(2)}, u32[]{:S(2)}) async-start(bf16[64,1,32,256]{3,2,1,0:T(8,128)(2,1)} %bitcast.1), calls=%async_computation.1 | async-start | bytes 2097152 | tf_op jit(solution)/shard_map/all_to_all | solution.py:52
  86.3 2.6 copy-start.5
  86.6 2.8 copy-start
  90.3 1.7 copy-start.1
  96.1 2.6 copy-start.5
  96.4 2.8 copy-start
  100.1 1.7 copy-start.1
  105.8 2.6 copy-start.5
  106.1 2.8 copy-start
  109.8 1.7 copy-start.1
  115.6 2.6 copy-start.5
  115.8 2.8 copy-start
  119.6 1.7 copy-start.1
  121.3 44.6 %copy-start.7 = (s32[1,64,32]{2,0,1:T(1,128)S(1)}, s32[1,64,32]{2,0,1:T(1,128)}, u32[]{:S(2)}) copy-start(s32[1,64,32]{2,0,1:T(1,128)} %copy-done.6) | copy-start | bytes 24580
  122.6 43.5 %copy-start.2 = (f32[8,8,32,32]{2,3,0,1:T(8,128)S(1)}, f32[8,8,32,32]{2,3,0,1:T(8,128)}, u32[]{:S(2)}) copy-start(f32[8,8,32,32]{2,3,0,1:T(8,128)} %get-tuple-element.138) | copy-start | bytes 786436
  160.2 35.3 %all-to-all-start.2 = ((bf16[64,1,1,32,256]{4,3,2,1,0:T(8,128)(2,1)}), bf16[64,1,1,32,256]{4,3,2,1,0:T(8,128)(2,1)S(1)}, u32[]{:S(2)}, u32[]{:S(2)}) async-start(bf16[64,1,1,32,256]{4,3,2,1,0:T(8,128)(2,1)} %constant_dynamic-update-slice_fusion), calls=%async_computation.2 | async-start | bytes 2097152 | tf_op jit(solution)/shard_map/all_to_all | solution.py:146
  165.9 1.6 copy-start.11
  165.9 193.4 %all-reduce.5.cloned.1.call-start = ((), (), s32[]{:S(2)}) async-start(), calls=%async_computation.4 | async-start | bytes 2097152 | tf_op jit(solution)/shard_map/psum | solution.py:160
  167.5 243.2 %all-reduce.3.cloned.1.call-start = ((), (), s32[]{:S(2)}) async-start(), calls=%async_computation.3 | async-start | bytes 2097152 | tf_op jit(solution)/shard_map/psum | solution.py:159
  207.7 1.0 copy-start.3
  359.4 53.6 %copy-start.4 = (f32[8,8,32,32]{3,2,1,0:T(8,128)S(1)}, f32[8,8,32,32]{3,2,1,0:T(8,128)}, u32[]{:S(2)}) copy-start(f32[8,8,32,32]{3,2,1,0:T(8,128)} %all-reduce.5.cloned.1.call-done) | copy-start | bytes 786436
Sparse Core Ops, SparseCore 0:
  170.2 189.1 all-reduce.4
  362.3 48.3 all-reduce.2
